TPU v7x, 32 devices: a whole 2x2x4 slice. The times are simulated.
32 devices in a mesh: graph: 8 (over y, x, core), dp: 4 (over z).
Axes of the slice: x: 2, y: 2, z: 4, core: 2. Of those that a mesh axis runs over, the one named last changes fastest.
Arguments:
- grid_latent: bfloat16 [4, 4096, 512], P('dp', 'graph'), may hold values from -6 to 6
- mesh_embed: bfloat16 [2048, 512], P('graph'), may hold values from -6 to 6
- mesh_edges: bfloat16 [12288, 512], P('graph'), may hold values from -6 to 6
- edge_geometry: bfloat16 [8, 4, 512], P('graph'), may hold values from -6 to 6
- edge_counts: int32 [8, 8], P('graph'), may hold values from 0 to 64, as said below
- edge_sources: int32 [8, 512], P('graph'), may hold values from 0 to 511
- edge_targets: int32 [8, 512], P('graph'), may hold values from 0 to 255
- halo_sources: int32 [8, 32], P('graph'), may hold values from 0 to 255
- mesh_sources: int32 [8, 1536], P('graph'), may hold values from 0 to 287, as said below
- mesh_targets: int32 [8, 1536], P('graph'), may hold values from 0 to 255
- grid_weight: bfloat16 [512, 512], replicated, may hold values from -0.25 to 0.25
- geometry_weight: float32 [4, 512], replicated, may hold values from -3 to 3
- message_weight: bfloat16 [512, 512], replicated, may hold values from -0.25 to 0.25
- mesh_update: bfloat16 [1024, 512], replicated, may hold values from -0.1875 to 0.1875
- mesh_output: bfloat16 [512, 512], replicated, may hold values from -0.25 to 0.25
- processor: bfloat16 [2, 3584, 512], replicated, may hold values from -0.15625 to 0.15625
- cotangent: bfloat16 [4, 2048, 512], P('dp', 'graph'), may hold values from -6 to 6
Outputs:
- mesh_result: bfloat16 [4, 2048, 512], P('dp', 'graph')
- mesh_gradient: bfloat16 [4, 2048, 512], P('dp', 'graph')
- gradients: bfloat16 [2, 3584, 512], replicated
Inputs may be any that keep to these rules, and one draw needn't show every extreme that they name: Slots of device s for device d beyond edge_counts[s, d] are empty; every device fills all 64 slots for itself, and every device fills all 64 slots for one common device. `edge_sources`: row s holds local grid rows of device s. `edge_targets`: row d holds local mesh rows of device d, for slot c from device s at column s * 64 + c. `halo_sources`: row s, columns d * 4 to d * 4 + 3 are the local rows that device s sends to device d; every device sends 4 rows to every device, itself included. `mesh_sources`: A value under 256 is a local row; a value 256 + s * 4 + k is halo slot k from device s.
All inputs are finite; a program needn't handle non-finite values.
Results may differ from a plain program's by a relative error of at most 0.024.
Values may be sent and summed in bfloat16 or wider, within the bound.
No kernel may reach another device: no remote copies, remote signals or barrier semaphores. Data moves between devices by JAX's collectives and lax.ppermute only.
A program may use at most 128 MiB of HBM per device.

v0:
```python
import math
import jax
import jax.numpy as jnp
from jax import lax
from jax.sharding import PartitionSpec as P

EPSILON = 1e-05
HIGHEST = lax.Precision.HIGHEST


def matmul(left, right):
    return jnp.dot(left, right, preferred_element_type=jnp.float32)


def weight_grad(left, right):
    return lax.dot_general(
        left, right, (((0,), (0,)), ((), ())), preferred_element_type=jnp.float32
    )


def input_grad(left, right):
    return lax.dot_general(
        left, right, (((1,), (1,)), ((), ())), preferred_element_type=jnp.float32
    )


def normalize(values):
    center = jnp.mean(values, axis=-1, keepdims=True)
    shifted = values - center
    inverse = lax.rsqrt(jnp.mean(shifted * shifted, axis=-1, keepdims=True) + EPSILON)
    return (shifted * inverse, inverse)


def normalize_back(normed, inverse, upstream):
    first_mean = jnp.mean(upstream, axis=-1, keepdims=True)
    second_mean = jnp.mean(upstream * normed, axis=-1, keepdims=True)
    return inverse * (upstream - first_mean - normed * second_mean)


def swish_slope(values):
    sigma = jax.nn.sigmoid(values)
    return sigma * (1.0 + values * (1.0 - sigma))


def member_table(indices, count_rows, dtype):
    rows_iota = lax.broadcasted_iota(jnp.int32, (count_rows, indices.shape[0]), 0)
    return (rows_iota == indices[None, :]).astype(dtype)


def on_device(
    grid_latent,
    mesh_embed,
    mesh_edges,
    edge_geometry,
    edge_counts,
    edge_sources,
    edge_targets,
    halo_sources,
    mesh_sources,
    mesh_targets,
    grid_weight,
    geometry_weight,
    message_weight,
    mesh_update,
    mesh_output,
    processor,
    cotangent,
):
    width = mesh_embed.shape[1]
    nodes_local = mesh_embed.shape[0]
    peers = lax.axis_size("graph")
    grid_rows = grid_latent[0]
    slots = edge_sources.shape[1]
    capacity = slots // peers
    position = lax.iota(jnp.int32, slots)
    column = position % capacity
    target_peer = position // capacity
    live = column < edge_counts[0][target_peer]
    geometry = edge_geometry[0]
    geometry_term = jnp.einsum(
        "fs,fd->sd", geometry.astype(jnp.float32), geometry_weight, precision=HIGHEST
    )
    grid_proj = matmul(grid_rows, grid_weight)
    messages = jnp.where(
        live[:, None], jax.nn.silu(grid_proj[edge_sources[0]] + geometry_term), 0.0
    ).astype(jnp.bfloat16)
    arrived = lax.all_to_all(messages, "graph", split_axis=0, concat_axis=0, tiled=True)
    hidden_sum = matmul(member_table(edge_targets[0], nodes_local, jnp.bfloat16), arrived).astype(
        jnp.bfloat16
    )
    aggregate = matmul(hidden_sum, message_weight).astype(jnp.bfloat16)
    pre_update = matmul(mesh_embed, mesh_update[:width]) + matmul(aggregate, mesh_update[width:])
    normed_start, inverse_start = normalize(
        matmul(jax.nn.silu(pre_update).astype(jnp.bfloat16), mesh_output)
    )
    nodes = (mesh_embed.astype(jnp.float32) + normed_start).astype(jnp.bfloat16)
    senders = mesh_sources[0]
    receivers = mesh_targets[0]
    halo_index = halo_sources[0]
    extended_rows = nodes_local + halo_index.shape[0]
    recv_table16 = member_table(receivers, nodes_local, jnp.bfloat16)
    edges = mesh_edges
    layers = processor.shape[0]
    stored = []
    for layer_index in range(layers):
        weights = processor[layer_index]
        incoming = lax.all_to_all(
            nodes[halo_index], "graph", split_axis=0, concat_axis=0, tiled=True
        )
        extended = jnp.concatenate([nodes, incoming], 0)
        send_proj = matmul(extended, weights[width : 2 * width])
        recv_proj = matmul(nodes, weights[2 * width : 3 * width])
        pre_edge = matmul(edges, weights[:width]) + send_proj[senders] + recv_proj[receivers]
        hidden_edge = jax.nn.silu(pre_edge).astype(jnp.bfloat16)
        normed_edge, inverse_edge = normalize(matmul(hidden_edge, weights[3 * width : 4 * width]))
        new_edges = (edges.astype(jnp.float32) + normed_edge).astype(jnp.bfloat16)
        summed = matmul(recv_table16, new_edges).astype(jnp.bfloat16)
        pre_node = matmul(nodes, weights[4 * width : 5 * width]) + matmul(
            summed, weights[5 * width : 6 * width]
        )
        hidden_node = jax.nn.silu(pre_node).astype(jnp.bfloat16)
        normed_node, inverse_node = normalize(matmul(hidden_node, weights[6 * width :]))
        new_nodes = (nodes.astype(jnp.float32) + normed_node).astype(jnp.bfloat16)
        stored.append(
            (
                nodes,
                edges,
                pre_edge,
                hidden_edge,
                normed_edge,
                inverse_edge,
                summed,
                pre_node,
                hidden_node,
                normed_node,
                inverse_node,
            )
        )
        nodes, edges = (new_nodes, new_edges)
    scale = 1.0 / math.sqrt(lax.axis_size("dp") * peers * nodes_local)
    grad_nodes = cotangent[0].astype(jnp.float32)
    grad_edges = jnp.zeros(edges.shape, jnp.float32)
    pieces = [None] * layers
    for layer_index in reversed(range(layers)):
        weights = processor[layer_index]
        (
            layer_nodes,
            layer_edges,
            pre_edge,
            hidden_edge,
            normed_edge,
            inverse_edge,
            summed,
            pre_node,
            hidden_node,
            normed_node,
            inverse_node,
        ) = stored[layer_index]
        q_node = normalize_back(normed_node, inverse_node, grad_nodes).astype(jnp.bfloat16)
        grad_node_second = weight_grad(hidden_node, q_node)
        d_node = (input_grad(q_node, weights[6 * width :]) * swish_slope(pre_node)).astype(
            jnp.bfloat16
        )
        grad_node_own = weight_grad(layer_nodes, d_node)
        grad_node_sum = weight_grad(summed, d_node)
        grad_summed = input_grad(d_node, weights[5 * width : 6 * width])
        edge_upstream = grad_edges + grad_summed[receivers]
        q_edge = normalize_back(normed_edge, inverse_edge, edge_upstream).astype(jnp.bfloat16)
        grad_edge_second = weight_grad(hidden_edge, q_edge)
        d_edge = input_grad(q_edge, weights[3 * width : 4 * width]) * swish_slope(pre_edge)
        d_edge16 = d_edge.astype(jnp.bfloat16)
        send_extended = jax.ops.segment_sum(d_edge, senders, num_segments=extended_rows)
        returned = lax.all_to_all(
            send_extended[nodes_local:].astype(jnp.bfloat16),
            "graph",
            split_axis=0,
            concat_axis=0,
            tiled=True,
        ).astype(jnp.float32)
        grad_send = (
            send_extended[:nodes_local]
            + jax.ops.segment_sum(returned, halo_index, num_segments=nodes_local)
        ).astype(jnp.bfloat16)
        grad_recv = jax.ops.segment_sum(d_edge, receivers, num_segments=nodes_local).astype(
            jnp.bfloat16
        )
        partial_value = (
            jnp.concatenate(
                [
                    weight_grad(layer_edges, d_edge16),
                    weight_grad(layer_nodes, grad_send),
                    weight_grad(layer_nodes, grad_recv),
                    grad_edge_second,
                    grad_node_own,
                    grad_node_sum,
                    grad_node_second,
                ],
                0,
            )
            * scale
        )
        grad_edges = edge_upstream + input_grad(d_edge16, weights[:width])
        grad_nodes = (
            grad_nodes
            + input_grad(d_node, weights[4 * width : 5 * width])
            + input_grad(grad_send, weights[width : 2 * width])
            + input_grad(grad_recv, weights[2 * width : 3 * width])
        )
        pieces[layer_index] = lax.psum(partial_value, ("graph", "dp")).astype(jnp.bfloat16)
    gradients = jnp.stack(pieces)
    return (nodes[None], grad_nodes.astype(jnp.bfloat16)[None], gradients)


def solution(mesh):
    in_specs = (
        P("dp", "graph", None),
        P("graph", None),
        P("graph", None),
        P("graph", None, None),
        P("graph", None),
        P("graph", None),
        P("graph", None),
        P("graph", None),
        P("graph", None),
        P("graph", None),
        P(),
        P(),
        P(),
        P(),
        P(),
        P(),
        P("dp", "graph", None),
    )
    out_specs = (P("dp", "graph", None), P("dp", "graph", None), P())
    return jax.shard_map(
        on_device, mesh=mesh, in_specs=in_specs, out_specs=out_specs, check_vma=False
    )
```

profile of v0, /device:TPU:0, one launch (start us, length us, event | category | flops | bytes accessed | tf_op | source)
XLA Modules:
  0.0 500.3 jit_solution(7372707361949194737)
XLA Ops:
  7.6 4.4 compare_select_fusion.4
  15.6 5.3 %all-to-all-start = ((bf16[8,64,512]{2,1,0:T(8,128)(2,1)}), bf16[8,64,512]{2,1,0:T(8,128)(2,1)S(1)}, u32[]{:S(2)}, u32[]{:S(2)}) async-start(bf16[8,64,512]{2,1,0:T(8,128)(2,1)} %bitcast.14), calls=%async_computation | async-start | bytes 1048576 | tf_op jit(solution)/shard_map/all_to_all | solution.py:87
  24.3 6.3 %all-to-all-done = bf16[8,64,512]{2,1,0:T(8,128)(2,1)S(1)} async-done(((bf16[8,64,512]{2,1,0:T(8,128)(2,1)}), bf16[8,64,512]{2,1,0:T(8,128)(2,1)S(1)}, u32[]{:S(2)}, u32[]{:S(2)}) %all-to-all-start) | async-done | bytes 524320 | tf_op jit(solution)/shard_map/all_to_all | solution.py:87
  43.3 4.9 gather_fusion.3
  49.6 5.0 gather_fusion.2
  54.5 4.5 fusion.2
  70.1 4.3 all-to-all-start.2
  76.6 4.9 gather_fusion.6
  82.9 5.0 gather_fusion.5
  87.9 4.1 fusion.1
  103.7 4.9 gather_fusion.7
  126.1 10.6 %scatter_custom_fusion = f32[288,512]{1,0:T(8,128)S(1)} fusion(s32[1536]{0:T(1024)S(1)} %reduce.6, f32[1536,512]{1,0:T(8,128)} %copy-done.31, f32[]{:T(128)} %constant.79.clone.1), kind=kCustom, calls=%fused_computation.193 | custom fusion | flops 786432 | bytes 590336 | tf_op jit(solution)/shard_map/scatter-add | solution.py:172
  137.3 4.2 all-to-all-start.3
  143.1 10.4 %scatter_custom_fusion.2 = f32[256,512]{1,0:T(8,128)S(1)} fusion(s32[1536]{0:T(1024)S(1)} %reduce.3, f32[1536,512]{1,0:T(8,128)} %copy-done.31, f32[]{:T(128)} %constant.79.clone.1), kind=kCustom, calls=%fused_computation.198 | custom fusion | flops 786432 | bytes 524800 | tf_op jit(solution)/shard_map/scatter-add | solution.py:184
  161.0 5.4 %gather_fusion.8 = f32[1536,512]{1,0:T(8,128)} fusion(f32[256,512]{1,0:T(8,128)S(1)} %fusion.54, s32[2048]{0:T(1024)S(1)} %get-tuple-element.31), kind=kCustom, calls=%fused_computation.8 | custom fusion | bytes 6297600 | tf_op jit(solution)/shard_map/gather | solution.py:167
  170.1 5.3 %fusion.143 = (f32[1536]{0:T(1024)S(1)}, f32[1536]{0:T(1024)S(1)}, f32[1536,512]{0,1:T(8,128)S(1)}) fusion(f32[1536]{0:T(1024)S(1)} %add_rsqrt_fusion.1, f32[1536,512]{0,1:T(8,128)S(1)} %copy-done.3, f32[1536]{0:T(1024)S(1)} %broadcast_multiply_fusion.7, f32[1536,512]{0,1:T(8,128)} %copy.29, f32[1536,512]{0,1:T(8,128)} %copy-done.4, ...), kind=kOutput, calls=%fused_computation.263 | convolution fusion | flops 811594752 | bytes 16277504 | tf_op jit(solution)/shard_map/dot_general | solution.py:22
  177.6 4.6 convolution_multiply_fusion
  182.2 10.6 %scatter_custom_fusion.3 = f32[288,512]{1,0:T(8,128)S(1)} fusion(s32[1536]{0:T(1024)S(1)} %reduce.6, f32[1536,512]{1,0:T(8,128)} %convolution_multiply_fusion, f32[]{:T(128)} %constant.79.clone.1), kind=kCustom, calls=%fused_computation.191 | custom fusion | flops 786432 | bytes 590336 | tf_op jit(solution)/shard_map/scatter-add | solution.py:172
  205.6 7.1 %broadcast_multiply_fusion = f32[3584,512]{1,0:T(8,128)} fusion(f32[3584,512]{1,0:T(8,128)} %convolution_dynamic-update-slice_fusion.3), kind=kLoop, calls=%fused_computation.18 | loop fusion | flops 1835008 | bytes 14680064 | tf_op jit(solution)/shard_map/mul | solution.py:188
  213.4 4.2 all-to-all-start.4
  219.0 10.4 %scatter_custom_fusion.5 = f32[256,512]{1,0:T(8,128)S(1)} fusion(s32[1536]{0:T(1024)S(1)} %reduce.3, f32[1536,512]{1,0:T(8,128)} %convolution_multiply_fusion, f32[]{:T(128)} %constant.79.clone.1), kind=kCustom, calls=%fused_computation.196 | custom fusion | flops 786432 | bytes 524800 | tf_op jit(solution)/shard_map/scatter-add | solution.py:184
  243.1 7.0 %broadcast_multiply_fusion.1 = f32[3584,512]{1,0:T(8,128)} fusion(f32[3584,512]{1,0:T(8,128)} %convolution_dynamic-update-slice_fusion.8), kind=kLoop, calls=%fused_computation.19 | loop fusion | flops 1835008 | bytes 14680064 | tf_op jit(solution)/shard_map/mul | solution.py:188
  250.1 243.1 %all-reduce.2 = (bf16[3584,512]{1,0:T(8,128)(2,1)}, bf16[3584,512]{1,0:T(8,128)(2,1)}) all-reduce(f32[3584,512]{1,0:T(8,128)} %broadcast_multiply_fusion, f32[3584,512]{1,0:T(8,128)} %broadcast_multiply_fusion.1), channel_id=1, replica_groups=mesh['graph'=8,'dp'=4] {'graph','dp'}, use_global_device_ids=true, to_apply=%region_25.26 | all-reduce | flops 3670016 | bytes 22020096 | tf_op jit(solution)/shard_map/psum | solution.py:209
  493.2 6.9 %pad_maximum_fusion = bf16[2,3584,512]{2,1,0:T(8,128)(2,1)} fusion(bf16[1,3584,512]{2,1,0:T(8,128)(2,1)} %bitcast.182, bf16[1,3584,512]{2,1,0:T(8,128)(2,1)} %bitcast.183), kind=kLoop, calls=%fused_computation.15 | loop fusion | flops 3670016 | bytes 14680064 | tf_op jit(solution)/shard_map/stack | solution.py:210
  (233 shorter events, 115.0 us)
Async XLA Ops:
  5.2 7.4 %copy-start.57 = (f32[4,512]{1,0:T(4,128)S(1)}, f32[4,512]{1,0:T(4,128)}, u32[]{:S(2)}) copy-start(f32[4,512]{1,0:T(4,128)} %param.28) | copy-start | bytes 24580
  5.2 7.4 %copy-start.58 = (bf16[1,4,512]{2,1,0:T(4,128)(2,1)S(1)}, bf16[1,4,512]{2,1,0:T(4,128)(2,1)}, u32[]{:S(2)}) copy-start(bf16[1,4,512]{2,1,0:T(4,128)(2,1)} %param.20) | copy-start | bytes 12292
  12.6 8.3 %copy-start.54 = (s32[1,1536]{1,0:T(1,128)S(1)}, s32[1,1536]{1,0:T(1,128)}, u32[]{:S(2)}) copy-start(s32[1,1536]{1,0:T(1,128)} %param.25) | copy-start | bytes 18436
  12.6 8.3 %copy-start.55 = (s32[1,1536]{1,0:T(1,128)S(1)}, s32[1,1536]{1,0:T(1,128)}, u32[]{:S(2)}) copy-start(s32[1,1536]{1,0:T(1,128)} %param.26) | copy-start | bytes 18436
  12.7 8.4 %copy-start.32 = (bf16[1,256,512]{2,1,0:T(8,128)(2,1)S(1)}, bf16[1,256,512]{2,1,0:T(8,128)(2,1)}, u32[]{:S(2)}) copy-start(bf16[1,256,512]{2,1,0:T(8,128)(2,1)} %param.33) | copy-start | bytes 786436
  15.6 7.4 %copy-start.42 = (bf16[256,512]{1,0:T(8,128)(2,1)S(1)}, bf16[256,512]{1,0:T(8,128)(2,1)}, u32[]{:S(2)}) copy-start(bf16[256,512]{1,0:T(8,128)(2,1)} %param.18) | copy-start | bytes 786436
  15.6 15.0 %copy-start.59 = (s32[1,512]{1,0:T(1,128)S(1)}, s32[1,512]{1,0:T(1,128)}, u32[]{:S(2)}) copy-start(s32[1,512]{1,0:T(1,128)} %param.23) | copy-start | bytes 6148
  15.6 15.0 %all-to-all-start = ((bf16[8,64,512]{2,1,0:T(8,128)(2,1)}), bf16[8,64,512]{2,1,0:T(8,128)(2,1)S(1)}, u32[]{:S(2)}, u32[]{:S(2)}) async-start(bf16[8,64,512]{2,1,0:T(8,128)(2,1)} %bitcast.14), calls=%async_computation | async-start | bytes 1048576 | tf_op jit(solution)/shard_map/all_to_all | solution.py:87
  36.5 11.7 %all-to-all-start.1 = ((bf16[8,4,512]{2,1,0:T(4,128)(2,1)}), bf16[8,4,512]{2,1,0:T(4,128)(2,1)S(1)}, u32[]{:S(2)}, u32[]{:S(2)}) async-start(bf16[8,4,512]{2,1,0:T(4,128)(2,1)} %all_to_all.39), calls=%async_computation.1 | async-start | bytes 65536 | tf_op jit(solution)/shard_map/all_to_all | solution.py:107
  67.1 14.4 %copy-start.9 = (f32[256,512]{1,0:T(8,128)}, f32[256,512]{1,0:T(8,128)S(1)}, u32[]{:S(2)}) copy-start(f32[256,512]{1,0:T(8,128)S(1)} %get-tuple-element.24) | copy-start | bytes 1572868
  67.5 32.3 %copy-start.7 = (bf16[256,512]{1,0:T(8,128)(2,1)}, bf16[256,512]{1,0:T(8,128)(2,1)S(1)}, u32[]{:S(2)}) copy-start(bf16[256,512]{1,0:T(8,128)(2,1)S(1)} %add_convert_fusion.6) | copy-start | bytes 786436
  70.1 11.4 %all-to-all-start.2 = ((bf16[8,4,512]{2,1,0:T(4,128)(2,1)}), bf16[8,4,512]{2,1,0:T(4,128)(2,1)S(1)}, u32[]{:S(2)}, u32[]{:S(2)}) async-start(bf16[8,4,512]{2,1,0:T(4,128)(2,1)} %all_to_all.42), calls=%async_computation.2 | async-start | bytes 65536 | tf_op jit(solution)/shard_map/all_to_all | solution.py:107
  94.6 7.6 %copy-start.5 = (f32[1536,512]{0,1:T(8,128)}, f32[1536,512]{0,1:T(8,128)S(1)}, u32[]{:S(2)}) copy-start(f32[1536,512]{0,1:T(8,128)S(1)} %get-tuple-element.26) | copy-start | bytes 9437188
  111.0 11.4 %copy-start.4 = (f32[1536,512]{0,1:T(8,128)}, f32[1536,512]{0,1:T(8,128)S(1)}, u32[]{:S(2)}) copy-start(f32[1536,512]{0,1:T(8,128)S(1)} %copy.26) | copy-start | bytes 9437188
  126.1 27.5 %copy-start.56 = (s32[1,32]{1,0:T(1,128)S(1)}, s32[1,32]{1,0:T(1,128)}, u32[]{:S(2)}) copy-start(s32[1,32]{1,0:T(1,128)} %param.24) | copy-start | bytes 388
  137.3 16.2 %all-to-all-start.3 = ((bf16[8,4,512]{2,1,0:T(4,128)(2,1)}), bf16[8,4,512]{2,1,0:T(4,128)(2,1)S(1)}, u32[]{:S(2)}, u32[]{:S(2)}) async-start(bf16[8,4,512]{2,1,0:T(4,128)(2,1)} %all_to_all.45), calls=%async_computation.3 | async-start | bytes 65536 | tf_op jit(solution)/shard_map/all_to_all | solution.py:173
  141.5 14.7 %copy-start.10 = (f32[256,512]{1,0:T(8,128)S(1)}, f32[256,512]{1,0:T(8,128)}, u32[]{:S(2)}) copy-start(f32[256,512]{1,0:T(8,128)} %copy-done.9) | copy-start | bytes 1572868
  177.6 15.2 %copy-start.13 = (bf16[1536,512]{1,0:T(8,128)(2,1)S(1)}, bf16[1536,512]{1,0:T(8,128)(2,1)}, u32[]{:S(2)}) copy-start(bf16[1536,512]{1,0:T(8,128)(2,1)} %param.19) | copy-start | bytes 4718596
  192.8 5.4 %copy-start.20 = (f32[256,512]{1,0:T(8,128)S(1)}, f32[256,512]{1,0:T(8,128)}, u32[]{:S(2)}) copy-start(f32[256,512]{1,0:T(8,128)} %copy-done.19) | copy-start | bytes 1572868
  192.8 6.7 %copy-start.39 = (bf16[1536,512]{0,1:T(8,128)(2,1)S(1)}, bf16[1536,512]{0,1:T(8,128)(2,1)}, u32[]{:S(2)}) copy-start(bf16[1536,512]{0,1:T(8,128)(2,1)} %copy-done.38) | copy-start | bytes 4718596
  205.6 12.0 %copy-start.18 = (f32[256,512]{1,0:T(8,128)S(1)}, f32[256,512]{1,0:T(8,128)}, u32[]{:S(2)}) copy-start(f32[256,512]{1,0:T(8,128)} %copy-done.17) | copy-start | bytes 1572868
  205.6 12.0 %copy-start.22 = (bf16[256,512]{1,0:T(8,128)(2,1)S(1)}, bf16[256,512]{1,0:T(8,128)(2,1)}, u32[]{:S(2)}) copy-start(bf16[256,512]{1,0:T(8,128)(2,1)} %copy-done.21) | copy-start | bytes 786436
  213.4 16.0 %all-to-all-start.4 = ((bf16[8,4,512]{2,1,0:T(4,128)(2,1)}), bf16[8,4,512]{2,1,0:T(4,128)(2,1)S(1)}, u32[]{:S(2)}, u32[]{:S(2)}) async-start(bf16[8,4,512]{2,1,0:T(4,128)(2,1)} %all_to_all.47), calls=%async_computation.4 | async-start | bytes 65536 | tf_op jit(solution)/shard_map/all_to_all | solution.py:173
  493.2 6.9 %copy-start.1 = (bf16[512,512]{1,0:T(8,128)(2,1)S(1)}, bf16[512,512]{1,0:T(8,128)(2,1)}, u32[]{:S(2)}) copy-start(bf16[512,512]{1,0:T(8,128)(2,1)} %param.27) | copy-start | bytes 1572868
  (41 other events, 137.7 us)
where the time goes:
time: 509 us; the launch traced here: 500 us
  blocking collectives  243 us (48%)
  matrix products  93.5 us (18%)
  other arithmetic  82.9 us (16%)
  local copies, waits for them, and re-layouts  51.2 us (10%)
  starting transfers between devices  21.4 us (4%)
  waiting for transfers between devices  6.35 us (1%)
    psum x1, blocking collectives, on_device(): lax.psum(partial_value, ('graph', 'dp')).astype(jnp.bfloat16)  243 us
    dot_general x20, matrix products, matmul(): return jnp.dot(left, right, preferred_element_type=jnp.float32)  38 us
    dot_general x13, matrix products, input_grad(): lax.dot_general(left, right, (((1,), (1,)), ((), ())), preferred_element_...  29.1 us
    dot_general x14, matrix products, weight_grad(): lax.dot_general(left, right, (((0,), (0,)), ((), ())), preferred_element_...  23.4 us
    scatter-add x2, other arithmetic, on_device(): jax.ops.segment_sum(d_edge, senders, num_segments=extended_rows)  21.2 us
    scatter-add x2, other arithmetic, on_device(): jax.ops.segment_sum(d_edge, receivers, num_segments=nodes_local)  20.7 us
    gather x4, local copies, waits for them, and re-layouts, on_device(): edge_upstream = grad_edges + grad_summed[receivers]  16.3 us
    mul x2, other arithmetic, on_device(): jnp.concatenate([weight_grad(layer_edges, d_edge16), weight_grad(layer_no...  14.1 us
  transfers between devices with their start and end apart: 5, of which 1 were waited for; matrix products, arithmetic and copies ran while one was open for 8% of the time, Pallas kernels for 0%

commit v1 on v0

--- a/solution.py
+++ b/solution.py
@@ -6,6 +6,29 @@
 
 EPSILON = 1e-05
 HIGHEST = lax.Precision.HIGHEST
+
+
+def cut_along(x, dim, peers):
+    lengths = x.shape
+    pieces = x.reshape(*lengths[:dim], peers, lengths[dim] // peers, *lengths[dim + 1 :])
+    return jnp.moveaxis(pieces, dim, 0)
+
+
+def laid_out(parts, dim):
+    parts = jnp.moveaxis(parts, 0, dim)
+    shape = parts.shape
+    return parts.reshape(*shape[:dim], shape[dim] * shape[dim + 1], *shape[dim + 2 :])
+
+
+def pairwise_exchange(x, axis, split_dim, concat_dim):
+    length, index = (lax.axis_size(axis), lax.axis_index(axis))
+    blocks = cut_along(x, split_dim, length)
+    done = [blocks[index]]
+    for step in range(1, length):
+        sent = blocks[index ^ step]
+        done.append(lax.ppermute(sent, axis, [(i, i ^ step) for i in range(length)]))
+    blocks = jnp.stack(done)[index ^ jnp.arange(length)]
+    return laid_out(blocks, concat_dim)
 
 
 def matmul(left, right):
@@ -84,7 +107,7 @@
     messages = jnp.where(
         live[:, None], jax.nn.silu(grid_proj[edge_sources[0]] + geometry_term), 0.0
     ).astype(jnp.bfloat16)
-    arrived = lax.all_to_all(messages, "graph", split_axis=0, concat_axis=0, tiled=True)
+    arrived = pairwise_exchange(messages, "graph", 0, 0)
     hidden_sum = matmul(member_table(edge_targets[0], nodes_local, jnp.bfloat16), arrived).astype(
         jnp.bfloat16
     )

time: 509 us -> 518 us (1.018)
  local copies, waits for them, and re-layouts: 51.2 us -> 57.5 us
    ppermute x0 -> x7, starting transfers between devices: none -> 8.37 us  [pairwise_exchange(): lax.ppermute(sent, axis, [(i, i ^ step) for i in range(length)])]
    all_to_all x1 -> x0, waiting for transfers between devices: 6.34 us -> none  [on_device(): lax.all_to_all(messages, 'graph', split_axis=0, concat_axis=0, tiled=True)]
    ppermute x0 -> x7, waiting for transfers between devices: none -> 5.4 us  [pairwise_exchange(): lax.ppermute(sent, axis, [(i, i ^ step) for i in range(length)])]
    all_to_all x1 -> x0, starting transfers between devices: 5.33 us -> none  [on_device(): lax.all_to_all(messages, 'graph', split_axis=0, concat_axis=0, tiled=True)]
    unnamed x121 -> x129, local copies, waits for them, and re-layouts: 7.25 us -> 10.6 us
  transfers between devices with their start and end apart: 5 -> 11, of which waited for: 1 -> 2; matrix products, arithmetic and copies ran while one was open for 8% -> 9% of each run, Pallas kernels for 0% -> 0%
where the time goes in v1:
time: 518 us; the launch traced here: 508 us
  blocking collectives  243 us (47%)
  matrix products  92.8 us (18%)
  other arithmetic  82.2 us (16%)
  local copies, waits for them, and re-layouts  57.5 us (11%)
  starting transfers between devices  25.1 us (5%)
  waiting for transfers between devices  5.42 us (1%)
    psum x1, blocking collectives, on_device(): lax.psum(partial_value, ('graph', 'dp')).astype(jnp.bfloat16)  243 us
    dot_general x20, matrix products, matmul(): return jnp.dot(left, right, preferred_element_type=jnp.float32)  38.2 us
    dot_general x13, matrix products, input_grad(): lax.dot_general(left, right, (((1,), (1,)), ((), ())), preferred_element_...  29.1 us
    dot_general x14, matrix products, weight_grad(): lax.dot_general(left, right, (((0,), (0,)), ((), ())), preferred_element_...  23.4 us
    scatter-add x2, other arithmetic, on_device(): jax.ops.segment_sum(d_edge, senders, num_segments=extended_rows)  21.2 us
    scatter-add x2, other arithmetic, on_device(): jax.ops.segment_sum(d_edge, receivers, num_segments=nodes_local)  20.7 us
    gather x4, local copies, waits for them, and re-layouts, on_device(): edge_upstream = grad_edges + grad_summed[receivers]  16.3 us
    mul x2, other arithmetic, on_device(): jnp.concatenate([weight_grad(layer_edges, d_edge16), weight_grad(layer_no...  14.1 us
  transfers between devices with their start and end apart: 11, of which 2 were waited for; matrix products, arithmetic and copies ran while one was open for 9% of the time, Pallas kernels for 0%

profile of v1, /device:TPU:0, one launch (start us, length us, event | category | flops | bytes accessed | tf_op | source)
XLA Modules:
  0.0 508.3 jit_solution(5928721985930046746)
XLA Ops:
  2.3 5.1 %compare_select_fusion.2 = (s32[512,1]{0,1:T(1,128)S(1)}, s32[512,1]{0,1:T(1,128)S(1)}) fusion(s32[1,512]{1,0:T(1,128)} %param.22, s32[]{:T(128)} %bitcast.8, s32[]{:T(128)} %bitcast.7, s32[]{:T(128)} %bitcast.6, s32[]{:T(128)} %bitcast.5, s32[]{:T(128)} %bitcast.4, s32[]{:T(128)} %bitcast.3, s32[]{:T(128)} %bitcast.2), kind=kLoop, calls=%fused_computation.230 | loop fusion | flops 13312 | bytes 6172 | tf_op jit(solution)/shard_map/select_n | solution.py:108
  43.8 4.0 all-to-all-start
  51.2 4.9 gather_fusion.4
  57.5 5.0 gather_fusion.3
  62.5 4.5 fusion.2
  78.0 4.4 all-to-all-start.1
  84.6 4.9 gather_fusion.7
  90.9 5.0 gather_fusion.6
  95.9 4.1 fusion.1
  111.7 4.9 gather_fusion.8
  134.1 10.6 %scatter_custom_fusion = f32[288,512]{1,0:T(8,128)S(1)} fusion(s32[1536]{0:T(1024)S(1)} %reduce.6, f32[1536,512]{1,0:T(8,128)} %copy-done.31, f32[]{:T(128)} %constant.94.clone.1), kind=kCustom, calls=%fused_computation.194 | custom fusion | flops 786432 | bytes 590336 | tf_op jit(solution)/shard_map/scatter-add | solution.py:195
  145.3 4.2 all-to-all-start.2
  151.1 10.4 %scatter_custom_fusion.2 = f32[256,512]{1,0:T(8,128)S(1)} fusion(s32[1536]{0:T(1024)S(1)} %reduce.3, f32[1536,512]{1,0:T(8,128)} %copy-done.31, f32[]{:T(128)} %constant.94.clone.1), kind=kCustom, calls=%fused_computation.199 | custom fusion | flops 786432 | bytes 524800 | tf_op jit(solution)/shard_map/scatter-add | solution.py:207
  169.0 5.4 %gather_fusion.9 = f32[1536,512]{1,0:T(8,128)} fusion(f32[256,512]{1,0:T(8,128)S(1)} %fusion.54, s32[2048]{0:T(1024)S(1)} %get-tuple-element.41), kind=kCustom, calls=%fused_computation.9 | custom fusion | bytes 6297600 | tf_op jit(solution)/shard_map/gather | solution.py:190
  178.1 5.3 %fusion.144 = (f32[1536]{0:T(1024)S(1)}, f32[1536]{0:T(1024)S(1)}, f32[1536,512]{0,1:T(8,128)S(1)}) fusion(f32[1536]{0:T(1024)S(1)} %add_rsqrt_fusion.1, f32[1536,512]{0,1:T(8,128)S(1)} %copy-done.3, f32[1536]{0:T(1024)S(1)} %broadcast_multiply_fusion.7, f32[1536,512]{0,1:T(8,128)} %copy.29, f32[1536,512]{0,1:T(8,128)} %copy-done.4, ...), kind=kOutput, calls=%fused_computation.282 | convolution fusion | flops 811594752 | bytes 16277504 | tf_op jit(solution)/shard_map/dot_general | solution.py:45
  185.5 4.6 convolution_multiply_fusion
  190.1 10.6 %scatter_custom_fusion.3 = f32[288,512]{1,0:T(8,128)S(1)} fusion(s32[1536]{0:T(1024)S(1)} %reduce.6, f32[1536,512]{1,0:T(8,128)} %convolution_multiply_fusion, f32[]{:T(128)} %constant.94.clone.1), kind=kCustom, calls=%fused_computation.192 | custom fusion | flops 786432 | bytes 590336 | tf_op jit(solution)/shard_map/scatter-add | solution.py:195
  200.7 4.1 fusion.12
  213.6 7.1 %broadcast_multiply_fusion = f32[3584,512]{1,0:T(8,128)} fusion(f32[3584,512]{1,0:T(8,128)} %convolution_dynamic-update-slice_fusion.3), kind=kLoop, calls=%fused_computation.19 | loop fusion | flops 1835008 | bytes 14680064 | tf_op jit(solution)/shard_map/mul | solution.py:211
  221.4 4.2 all-to-all-start.3
  226.9 10.4 %scatter_custom_fusion.5 = f32[256,512]{1,0:T(8,128)S(1)} fusion(s32[1536]{0:T(1024)S(1)} %reduce.3, f32[1536,512]{1,0:T(8,128)} %convolution_multiply_fusion, f32[]{:T(128)} %constant.94.clone.1), kind=kCustom, calls=%fused_computation.197 | custom fusion | flops 786432 | bytes 524800 | tf_op jit(solution)/shard_map/scatter-add | solution.py:207
  251.1 7.0 %broadcast_multiply_fusion.1 = f32[3584,512]{1,0:T(8,128)} fusion(f32[3584,512]{1,0:T(8,128)} %convolution_dynamic-update-slice_fusion.8), kind=kLoop, calls=%fused_computation.20 | loop fusion | flops 1835008 | bytes 14680064 | tf_op jit(solution)/shard_map/mul | solution.py:211
  258.1 243.1 %all-reduce.2 = (bf16[3584,512]{1,0:T(8,128)(2,1)}, bf16[3584,512]{1,0:T(8,128)(2,1)}) all-reduce(f32[3584,512]{1,0:T(8,128)} %broadcast_multiply_fusion, f32[3584,512]{1,0:T(8,128)} %broadcast_multiply_fusion.1), channel_id=1, replica_groups=mesh['graph'=8,'dp'=4] {'graph','dp'}, use_global_device_ids=true, to_apply=%region_25.26 | all-reduce | flops 3670016 | bytes 22020096 | tf_op jit(solution)/shard_map/psum | solution.py:232
  501.1 6.9 %pad_maximum_fusion = bf16[2,3584,512]{2,1,0:T(8,128)(2,1)} fusion(bf16[1,3584,512]{2,1,0:T(8,128)(2,1)} %bitcast.212, bf16[1,3584,512]{2,1,0:T(8,128)(2,1)} %bitcast.213), kind=kLoop, calls=%fused_computation.16 | loop fusion | flops 3670016 | bytes 14680064 | tf_op jit(solution)/shard_map/stack | solution.py:233
  (258 shorter events, 125.7 us)
Async XLA Ops:
  12.0 8.7 %copy-start.55 = (s32[1,1536]{1,0:T(1,128)S(1)}, s32[1,1536]{1,0:T(1,128)}, u32[]{:S(2)}) copy-start(s32[1,1536]{1,0:T(1,128)} %param.25) | copy-start | bytes 18436
  12.0 8.7 %copy-start.56 = (s32[1,1536]{1,0:T(1,128)S(1)}, s32[1,1536]{1,0:T(1,128)}, u32[]{:S(2)}) copy-start(s32[1,1536]{1,0:T(1,128)} %param.26) | copy-start | bytes 18436
  12.0 8.8 %copy-start.57 = (s32[1,32]{1,0:T(1,128)S(1)}, s32[1,32]{1,0:T(1,128)}, u32[]{:S(2)}) copy-start(s32[1,32]{1,0:T(1,128)} %param.24) | copy-start | bytes 388
  12.1 8.8 %copy-start.32 = (bf16[1,256,512]{2,1,0:T(8,128)(2,1)S(1)}, bf16[1,256,512]{2,1,0:T(8,128)(2,1)}, u32[]{:S(2)}) copy-start(bf16[1,256,512]{2,1,0:T(8,128)(2,1)} %param.33) | copy-start | bytes 786436
  14.9 13.9 %copy-start.54 = (bf16[64,512]{1,0:T(8,128)(2,1)S(1)}, bf16[64,512]{1,0:T(8,128)(2,1)}, u32[]{:S(2)}) copy-start(bf16[64,512]{1,0:T(8,128)(2,1)} %get-tuple-element.15) | copy-start | bytes 196612
  14.9 20.6 %collective-permute-start.6 = (bf16[64,512]{1,0:T(8,128)(2,1)S(1)}, bf16[64,512]{1,0:T(8,128)(2,1)}, u32[]{:S(2)}, u32[]{:S(2)}) collective-permute-start(bf16[64,512]{1,0:T(8,128)(2,1)S(1)} %get-tuple-element.11), channel_id=1, source_target_pairs={{0,28},{4,24},{8,20},{12,16},{16,12},{20,8},{24,4},{28,0},{1,29},{... | collective-permute-start | bytes 196616 | tf_op jit(solution)/shard_map/ppermute | solution.py:29
  18.3 16.4 %collective-permute-start.5 = (bf16[64,512]{1,0:T(8,128)(2,1)S(1)}, bf16[64,512]{1,0:T(8,128)(2,1)}, u32[]{:S(2)}, u32[]{:S(2)}) collective-permute-start(bf16[64,512]{1,0:T(8,128)(2,1)S(1)} %get-tuple-element.12), channel_id=1, source_target_pairs={{0,24},{4,28},{8,16},{12,20},{16,8},{20,12},{24,0},{28,4},{1,25},{... | collective-permute-start | bytes 196616 | tf_op jit(solution)/shard_map/ppermute | solution.py:29
  18.8 15.0 %collective-permute-start.4 = (bf16[64,512]{1,0:T(8,128)(2,1)S(1)}, bf16[64,512]{1,0:T(8,128)(2,1)}, u32[]{:S(2)}, u32[]{:S(2)}) collective-permute-start(bf16[64,512]{1,0:T(8,128)(2,1)S(1)} %get-tuple-element.13), channel_id=1, source_target_pairs={{0,20},{4,16},{8,28},{12,24},{16,4},{20,0},{24,12},{28,8},{1,21},{... | collective-permute-start | bytes 196616 | tf_op jit(solution)/shard_map/ppermute | solution.py:29
  20.3 12.7 %collective-permute-start.3 = (bf16[64,512]{1,0:T(8,128)(2,1)S(1)}, bf16[64,512]{1,0:T(8,128)(2,1)}, u32[]{:S(2)}, u32[]{:S(2)}) collective-permute-start(bf16[64,512]{1,0:T(8,128)(2,1)S(1)} %get-tuple-element.14), channel_id=1, source_target_pairs={{0,16},{4,20},{8,24},{12,28},{16,0},{20,4},{24,8},{28,12},{1,17},{... | collective-permute-start | bytes 196616 | tf_op jit(solution)/shard_map/ppermute | solution.py:29
  20.6 3.5 collective-permute-start
  21.0 16.7 %copy-start.60 = (s32[1,512]{1,0:T(1,128)S(1)}, s32[1,512]{1,0:T(1,128)}, u32[]{:S(2)}) copy-start(s32[1,512]{1,0:T(1,128)} %param.23) | copy-start | bytes 6148
  24.1 4.7 collective-permute-start.1
  28.8 4.2 collective-permute-start.2
  43.8 12.4 %all-to-all-start = ((bf16[8,4,512]{2,1,0:T(4,128)(2,1)}), bf16[8,4,512]{2,1,0:T(4,128)(2,1)S(1)}, u32[]{:S(2)}, u32[]{:S(2)}) async-start(bf16[8,4,512]{2,1,0:T(4,128)(2,1)} %all_to_all.28), calls=%async_computation | async-start | bytes 65536 | tf_op jit(solution)/shard_map/all_to_all | solution.py:130
  75.0 14.5 %copy-start.9 = (f32[256,512]{1,0:T(8,128)}, f32[256,512]{1,0:T(8,128)S(1)}, u32[]{:S(2)}) copy-start(f32[256,512]{1,0:T(8,128)S(1)} %get-tuple-element.32) | copy-start | bytes 1572868
  75.4 32.3 %copy-start.7 = (bf16[256,512]{1,0:T(8,128)(2,1)}, bf16[256,512]{1,0:T(8,128)(2,1)S(1)}, u32[]{:S(2)}) copy-start(bf16[256,512]{1,0:T(8,128)(2,1)S(1)} %add_convert_fusion.6) | copy-start | bytes 786436
  78.0 11.5 %all-to-all-start.1 = ((bf16[8,4,512]{2,1,0:T(4,128)(2,1)}), bf16[8,4,512]{2,1,0:T(4,128)(2,1)S(1)}, u32[]{:S(2)}, u32[]{:S(2)}) async-start(bf16[8,4,512]{2,1,0:T(4,128)(2,1)} %all_to_all.31), calls=%async_computation.1 | async-start | bytes 65536 | tf_op jit(solution)/shard_map/all_to_all | solution.py:130
  119.0 11.4 %copy-start.4 = (f32[1536,512]{0,1:T(8,128)}, f32[1536,512]{0,1:T(8,128)S(1)}, u32[]{:S(2)}) copy-start(f32[1536,512]{0,1:T(8,128)S(1)} %copy.26) | copy-start | bytes 9437188
  145.3 16.2 %all-to-all-start.2 = ((bf16[8,4,512]{2,1,0:T(4,128)(2,1)}), bf16[8,4,512]{2,1,0:T(4,128)(2,1)S(1)}, u32[]{:S(2)}, u32[]{:S(2)}) async-start(bf16[8,4,512]{2,1,0:T(4,128)(2,1)} %all_to_all.34), calls=%async_computation.2 | async-start | bytes 65536 | tf_op jit(solution)/shard_map/all_to_all | solution.py:196
  149.5 14.7 %copy-start.10 = (f32[256,512]{1,0:T(8,128)S(1)}, f32[256,512]{1,0:T(8,128)}, u32[]{:S(2)}) copy-start(f32[256,512]{1,0:T(8,128)} %copy-done.9) | copy-start | bytes 1572868
  185.5 15.2 %copy-start.13 = (bf16[1536,512]{1,0:T(8,128)(2,1)S(1)}, bf16[1536,512]{1,0:T(8,128)(2,1)}, u32[]{:S(2)}) copy-start(bf16[1536,512]{1,0:T(8,128)(2,1)} %param.19) | copy-start | bytes 4718596
  213.6 12.0 %copy-start.18 = (f32[256,512]{1,0:T(8,128)S(1)}, f32[256,512]{1,0:T(8,128)}, u32[]{:S(2)}) copy-start(f32[256,512]{1,0:T(8,128)} %copy-done.17) | copy-start | bytes 1572868
  213.6 12.0 %copy-start.22 = (bf16[256,512]{1,0:T(8,128)(2,1)S(1)}, bf16[256,512]{1,0:T(8,128)(2,1)}, u32[]{:S(2)}) copy-start(bf16[256,512]{1,0:T(8,128)(2,1)} %copy-done.21) | copy-start | bytes 786436
  221.4 16.0 %all-to-all-start.3 = ((bf16[8,4,512]{2,1,0:T(4,128)(2,1)}), bf16[8,4,512]{2,1,0:T(4,128)(2,1)S(1)}, u32[]{:S(2)}, u32[]{:S(2)}) async-start(bf16[8,4,512]{2,1,0:T(4,128)(2,1)} %all_to_all.36), calls=%async_computation.3 | async-start | bytes 65536 | tf_op jit(solution)/shard_map/all_to_all | solution.py:196
  (48 other events, 182.6 us)
